TPU v7x, 512 devices: a whole 4x4x16 slice. The times are simulated.
512 devices in a mesh: dp: 8 (over y, core), expert: 64 (over x, z).
Axes of the slice: x: 4, y: 4, z: 16, core: 2. Of those that a mesh axis runs over, the one named last changes fastest.
Arguments:
- pre_query: bfloat16 [8192, 16, 576], P(('dp', 'expert')), may hold values from -25 to 25
- pre_latent: bfloat16 [8192, 576], P(('dp', 'expert')), may hold values from -5 to 5
- pre_resid: bfloat16 [8192, 2048], P(('dp', 'expert')), may hold values from -6 to 6
- dec_query: bfloat16 [512, 16, 576], P(('dp', 'expert')), may hold values from -25 to 25
- dec_latent: bfloat16 [512, 576], P(('dp', 'expert')), may hold values from -5 to 5
- dec_resid: bfloat16 [512, 2048], P(('dp', 'expert')), may hold values from -6 to 6
- cache_lengths: int32 [512], P(('dp', 'expert')), may hold values from 1 to 32768
- latent_cache: bfloat16 [512, 1024, 576], P(('dp', 'expert')), may hold values from -5 to 5
- sink_logits: float32 [16], replicated, may hold values from -1 to 3
- uv_weight: bfloat16 [16, 512, 128], P('dp', 'expert'), may hold values from -0.25 to 0.25
- out_weight: bfloat16 [16, 128, 2048], P('dp', 'expert'), may hold values from -0.125 to 0.125
- norm_gain: bfloat16 [2048], replicated, may hold values from 0.5 to 1.5
- router: bfloat16 [2048, 64], P(None, 'expert'), may hold values from -0.125 to 0.125
- routes: int32 [8704, 6], P(('dp', 'expert')), may hold values from 0 to 63, all different within a row; in each aligned block of 17 rows (0 to 16, 17 to 33, ...) at most 2 rows name the same one
- gate_weight: bfloat16 [64, 2048, 1408], P('expert', None, 'dp'), may hold values from -0.125 to 0.125
- up_weight: bfloat16 [64, 2048, 1408], P('expert', None, 'dp'), may hold values from -0.125 to 0.125
- down_weight: bfloat16 [64, 1408, 2048], P('expert', None, 'dp'), may hold values from -0.15625 to 0.15625
- shared_gate: bfloat16 [2048, 1408], P('expert', 'dp'), may hold values from -0.125 to 0.125
- shared_up: bfloat16 [2048, 1408], P('expert', 'dp'), may hold values from -0.125 to 0.125
- shared_down: bfloat16 [1408, 2048], P('expert', 'dp'), may hold values from -0.15625 to 0.15625
Outputs:
- pre_out: bfloat16 [8192, 2048], P(('dp', 'expert'))
- dec_out: bfloat16 [512, 2048], P(('dp', 'expert'))
Inputs may be any that keep to these rules, and one draw needn't show every extreme that they name: `routes`: each row names 6 different experts; in each aligned block of 17 rows no expert is named by more than 2 rows.
All inputs are finite; a program needn't handle non-finite values.
Results may differ from a plain program's by a relative error of at most 0.015.
Values may be sent and summed in bfloat16 or wider, within the bound.
A program may use at most 64 MiB of HBM per device.

v0:
```python
from functools import partial
import jax
import jax.numpy as jnp
from jax import lax
from jax.sharding import PartitionSpec as P

D = 2048
LATENT = 512
ROPE = 64
QK_NOPE = 128
TOPK = 6
ROUTE_SCALE = 2.446
NORM_EPS = 1e-06
NEG_FILL = -1e30


def assign_slots(route_rows, experts):
    flat_routes = route_rows.reshape(-1)
    one_hot = (flat_routes[:, None] == jnp.arange(experts, dtype=jnp.int32)[None, :]).astype(
        jnp.int32
    )
    running = jnp.cumsum(one_hot, axis=0)
    slot_rank = jnp.sum(running * one_hot, axis=1) - 1
    return slot_rank.reshape(route_rows.shape)


def dispatch_matrix(route_rows, slot_rows, experts, capacity):
    target = route_rows * capacity + slot_rows
    places = jnp.arange(experts * capacity, dtype=jnp.int32)
    total = jnp.zeros((route_rows.shape[0], experts * capacity), jnp.bfloat16)
    for column in range(route_rows.shape[1]):
        total = total + (target[:, column][:, None] == places[None, :]).astype(jnp.bfloat16)
    return total


def gather_weights(members, **parts):
    names = list(parts)
    flat = jnp.concatenate([parts[n][0].reshape(-1) for n in names])
    lanes = 128
    total = flat.shape[0]
    padded = -(-total // lanes) * lanes
    flat = jnp.pad(flat, (0, padded - total)).reshape(1, padded // lanes, lanes)
    everyone = lax.all_gather(flat, "expert", axis=0, tiled=True).reshape(members, padded)
    out = {}
    start = 0
    for n in names:
        local, axis = parts[n]
        size = local.size
        piece = everyone[:, start : start + size].reshape((members,) + local.shape)
        piece = jnp.moveaxis(piece, 0, axis)
        shape = list(local.shape)
        shape[axis] *= members
        out[n] = piece.reshape(shape)
        start += size
    return out


def shards(
    pre_query,
    pre_latent,
    pre_resid,
    dec_query,
    dec_latent,
    dec_resid,
    cache_lengths,
    latent_cache,
    sink_logits,
    uv_weight,
    out_weight,
    norm_gain,
    router,
    routes,
    gate_weight,
    up_weight,
    down_weight,
    shared_gate,
    shared_up,
    shared_down,
):
    groups = lax.axis_size("dp")
    members = lax.axis_size("expert")
    pre_rows = pre_query.shape[0]
    rows_dev = pre_rows + 1
    scale_qk = (QK_NOPE + ROPE) ** (-0.5)
    weights = gather_weights(
        members,
        uv=(uv_weight, 1),
        out=(out_weight, 1),
        shared_gate=(shared_gate, 0),
        shared_up=(shared_up, 0),
        shared_down=(shared_down, 0),
    )
    pre_scores = (
        jnp.einsum("thc,uc->thu", pre_query, pre_latent, preferred_element_type=jnp.float32)
        * scale_qk
    )
    places = jnp.arange(pre_rows, dtype=jnp.int32)
    allowed = (places[None, :] <= places[:, None])[:, None, :]
    masked = jnp.where(allowed, pre_scores, NEG_FILL)
    pre_max = jnp.maximum(jnp.max(masked, axis=2), sink_logits[None, :])
    exp_terms = jnp.where(allowed, jnp.exp(masked - pre_max[:, :, None]), 0.0)
    denominator = jnp.sum(exp_terms, axis=2) + jnp.exp(sink_logits[None, :] - pre_max)
    numerator = jnp.einsum(
        "thu,ul->thl",
        exp_terms.astype(jnp.bfloat16),
        pre_latent[:, :LATENT],
        preferred_element_type=jnp.float32,
    )
    pre_att = (numerator / denominator[:, :, None]).astype(jnp.bfloat16)
    window = latent_cache.shape[1]
    slot_ids = jnp.arange(window, dtype=jnp.int32)
    newest = cache_lengths - 1
    position = newest[:, None] - jnp.mod(newest[:, None] - slot_ids[None, :], window)
    usable = ((position >= 0) & (position > cache_lengths[:, None] - window))[:, None, :]
    cache_scores = (
        jnp.einsum("rhc,rsc->rhs", dec_query, latent_cache, preferred_element_type=jnp.float32)
        * scale_qk
    )
    own_scores = (
        jnp.einsum("rhc,rc->rh", dec_query, dec_latent, preferred_element_type=jnp.float32)
        * scale_qk
    )
    cache_masked = jnp.where(usable, cache_scores, NEG_FILL)
    top_score = jnp.maximum(
        jnp.maximum(jnp.max(cache_masked, axis=2), own_scores), sink_logits[None, :]
    )
    cache_exp = jnp.where(usable, jnp.exp(cache_masked - top_score[:, :, None]), 0.0)
    own_exp = jnp.exp(own_scores - top_score)
    dec_numer = jnp.einsum(
        "rhs,rsl->rhl",
        cache_exp.astype(jnp.bfloat16),
        latent_cache[:, :, :LATENT],
        preferred_element_type=jnp.float32,
    )
    dec_numer = dec_numer + own_exp.astype(jnp.bfloat16).astype(jnp.float32)[
        :, :, None
    ] * dec_latent[:, None, :LATENT].astype(jnp.float32)
    dec_total = jnp.sum(cache_exp, axis=2) + own_exp + jnp.exp(sink_logits[None, :] - top_score)
    dec_att = (dec_numer / dec_total[:, :, None]).astype(jnp.bfloat16)
    attention = jnp.concatenate([pre_att, dec_att], axis=0)
    spread = lax.all_to_all(attention, "dp", split_axis=1, concat_axis=0, tiled=True)
    uv_full, out_full = (weights["uv"], weights["out"])
    head_values = jnp.einsum(
        "thl,hlv->thv", spread, uv_full, preferred_element_type=jnp.float32
    ).astype(jnp.bfloat16)
    head_partial = jnp.einsum(
        "thv,hvd->td", head_values, out_full, preferred_element_type=jnp.float32
    )
    attn_out = lax.psum_scatter(
        head_partial.astype(jnp.bfloat16), "dp", scatter_dimension=0, tiled=True
    ).astype(jnp.float32)
    resid = jnp.concatenate([pre_resid, dec_resid], axis=0)
    hidden = (resid.astype(jnp.float32) + attn_out).astype(jnp.bfloat16)
    hidden_up = lax.optimization_barrier(hidden).astype(jnp.float32)
    mean_square = jnp.mean(hidden_up * hidden_up, axis=1, keepdims=True)
    normed = (
        hidden_up * lax.rsqrt(mean_square + NORM_EPS) * norm_gain.astype(jnp.float32)[None, :]
    ).astype(jnp.bfloat16)
    capacity = max(2, (rows_dev * TOPK + members - 1) // members)
    group_tokens = lax.all_gather(normed, "dp", axis=0, tiled=True)
    group_routes = lax.all_gather(routes, "dp", axis=0, tiled=True)
    routes_by_group = group_routes.reshape(groups, rows_dev, TOPK)
    slots_by_group = jax.vmap(partial(assign_slots, experts=members))(routes_by_group)
    tokens_by_group = group_tokens.reshape(groups, rows_dev, D)
    all_matrix = jax.vmap(partial(dispatch_matrix, experts=members, capacity=capacity))(
        routes_by_group, slots_by_group
    )
    all_matrix = all_matrix.reshape(groups, rows_dev, members, capacity)
    outgoing = jnp.einsum(
        "grxc,grd->xgcd", all_matrix, tokens_by_group, preferred_element_type=jnp.bfloat16
    )
    expert_rows = lax.all_to_all(outgoing, "expert", split_axis=0, concat_axis=0, tiled=True)
    expert_rows = expert_rows.reshape(-1, D)
    gate_score = jax.nn.sigmoid(
        jnp.dot(expert_rows, router[:, 0], preferred_element_type=jnp.float32)
    )
    gate_proj = jnp.dot(expert_rows, gate_weight[0], preferred_element_type=jnp.float32)
    up_proj = jnp.dot(expert_rows, up_weight[0], preferred_element_type=jnp.float32)
    expert_act = (jax.nn.silu(gate_proj) * up_proj).astype(jnp.bfloat16)
    shared_gate_full, shared_up_full, shared_down_full = (
        weights["shared_gate"],
        weights["shared_up"],
        weights["shared_down"],
    )
    shared_act = (
        jax.nn.silu(jnp.dot(group_tokens, shared_gate_full, preferred_element_type=jnp.float32))
        * jnp.dot(group_tokens, shared_up_full, preferred_element_type=jnp.float32)
    ).astype(jnp.bfloat16)
    down_local = down_weight[0]
    col_width = down_local.shape[1]
    routed_piece = lax.all_gather(expert_act, "dp", axis=1, tiled=True)
    shared_piece = lax.all_gather(shared_act, "dp", axis=1, tiled=True)
    routed_cols = jnp.dot(routed_piece, down_local, preferred_element_type=jnp.float32)
    shared_cols = jnp.dot(shared_piece, shared_down_full, preferred_element_type=jnp.float32)
    expert_out = routed_cols.astype(jnp.bfloat16)
    shared_out = shared_cols.astype(jnp.bfloat16)
    returned = lax.all_to_all(
        expert_out.reshape(members, groups * capacity, col_width),
        "expert",
        split_axis=0,
        concat_axis=0,
        tiled=True,
    )
    returned_scores = lax.all_to_all(
        gate_score.reshape(members, groups * capacity),
        "expert",
        split_axis=0,
        concat_axis=0,
        tiled=True,
    )
    group_offset = (jnp.arange(groups, dtype=jnp.int32) * capacity)[:, None, None]
    lookup = (routes_by_group * (groups * capacity) + group_offset + slots_by_group).reshape(
        groups * rows_dev, TOPK
    )
    picked = jnp.take(returned.reshape(-1, col_width), lookup, axis=0)
    picked_scores = jnp.take(returned_scores.reshape(-1), lookup, axis=0)
    route_weight = ROUTE_SCALE * picked_scores / jnp.sum(picked_scores, axis=1, keepdims=True)
    moe_cols = shared_out.astype(jnp.float32) + jnp.sum(
        route_weight[:, :, None] * picked.astype(jnp.float32), axis=1
    )
    moe_home = lax.all_to_all(
        moe_cols.reshape(groups, rows_dev, col_width).astype(jnp.bfloat16),
        "dp",
        split_axis=0,
        concat_axis=2,
        tiled=True,
    ).astype(jnp.float32)
    final = (hidden_up + moe_home[0]).astype(jnp.bfloat16)
    return (final[:pre_rows], final[pre_rows:])


def solution(mesh):
    in_specs = (
        P(("dp", "expert"), None, None),
        P(("dp", "expert"), None),
        P(("dp", "expert"), None),
        P(("dp", "expert"), None, None),
        P(("dp", "expert"), None),
        P(("dp", "expert"), None),
        P(("dp", "expert")),
        P(("dp", "expert"), None, None),
        P(),
        P("dp", "expert", None),
        P("dp", "expert", None),
        P(),
        P(None, "expert"),
        P(("dp", "expert"), None),
        P("expert", None, "dp"),
        P("expert", None, "dp"),
        P("expert", None, "dp"),
        P("expert", "dp"),
        P("expert", "dp"),
        P("expert", "dp"),
    )
    out_specs = (P(("dp", "expert"), None), P(("dp", "expert"), None))
    return jax.shard_map(shards, mesh=mesh, in_specs=in_specs, out_specs=out_specs, check_vma=False)
```

profile of v0, /device:TPU:1, one launch (start us, length us, event | category | flops | bytes accessed | tf_op | source)
XLA Modules:
  0.0 537.1 jit_solution(8622716932991419900)
XLA Ops:
  7.2 0.9 reshape.278
  8.1 0.8 reshape.279
  8.9 0.7 reshape.280
  9.7 0.7 copy.105
  10.4 0.7 bitcast_dynamic-update-slice_fusion
  11.4 0.4 dynamic-update-slice.3
  11.8 0.6 copy-done.4
  13.2 1.7 fusion.83
  14.8 0.9 convert_convert_fusion
  15.9 1.6 fusion.84
  17.5 0.7 broadcast_maximum_fusion
  18.3 0.7 exponential_add_fusion.1
  18.9 0.7 slice_convert_fusion
  19.6 1.6 fusion.21
  21.3 0.4 fusion.3
  21.7 0.9 copy.83
  22.6 10.2 %all-to-all-start = ((bf16[17,16,512]{2,0,1:T(8,128)(2,1)}), bf16[17,16,512]{2,0,1:T(8,128)(2,1)S(1)}, u32[]{:S(2)}, u32[]{:S(2)}) async-start(bf16[17,16,512]{2,0,1:T(8,128)(2,1)} %copy.83), calls=%async_computation | async-start | bytes 786432 | tf_op jit(solution)/shard_map/all_to_all | solution.py:141
  32.8 14.7 %all-gather.2 = s32[8,17,6]{1,2,0:T(8,128)S(1)} all-gather(s32[1,17,6]{1,2,0:T(8,128)S(1)} %bitcast.151), channel_id=1, replica_groups=mesh['dp'=8,'expert'=64] {'dp'}, dimensions={0}, use_global_device_ids=true | all-gather | bytes 3672 | tf_op jit(solution)/shard_map/all_gather | solution.py:161
  47.8 2.0 select_reduce_fusion
  50.0 1.0 slice_reduce_fusion.5
  51.3 103.2 %all-gather.6.cloned.1.call-done = bf16[64,212,128]{2,1,0:T(8,128)(2,1)} async-done(((bf16[1,212,128]{2,1,0:T(8,128)(2,1)}), bf16[64,212,128]{2,1,0:T(8,128)(2,1)}) %all-gather.6.cloned.1.call-update) | async-done | bytes 3473424 | tf_op jit(solution)/shard_map/all_gather | solution.py:43
  154.5 2.4 copy.120
  157.0 1.8 copy-done.2
  158.9 0.8 reshape.289
  159.8 1.7 copy.86
  161.5 1.5 reshape.290
  162.9 0.5 fusion.1
  163.4 23.4 %fusion = bf16[24,2048]{1,0:T(8,128)(2,1)S(1)} fusion(bf16[136,2048]{1,0:T(8,128)(2,1)S(1)} %fusion.1), kind=kCustom, calls=%all-reduce-scatter | all-reduce-scatter fusion | flops 393217 | bytes 657408
  186.9 1.3 collective-permute-start.1
  188.2 4.5 collective-permute-start
  192.7 4.5 collective-permute-start.2
  197.2 1.3 dynamic-slice.4
  199.2 0.6 concatenate.12
  200.1 13.8 %all-gather = bf16[8,17,2048]{2,1,0:T(8,128)(2,1)S(1)} all-gather(bf16[1,17,2048]{2,1,0:T(8,128)(2,1)S(1)} %fusion.51), channel_id=1, replica_groups=mesh['dp'=8,'expert'=64] {'dp'}, dimensions={0}, use_global_device_ids=true | all-gather | bytes 626688 | tf_op jit(solution)/shard_map/all_gather | solution.py:160
  213.9 1.4 convolution_bitcast_fusion
  215.3 6.3 %copy.94 = bf16[64,8,2,2048]{3,2,1,0:T(2,128)(2,1)} copy(bf16[64,8,2,2048]{3,0,2,1:T(8,128)(2,1)S(1)} %convolution_bitcast_fusion) | data formatting | bytes 8388608 | tf_op jit(solution)/shard_map/grxc,grd->xgcd/transpose | solution.py:169
  221.6 191.1 %all_to_all.46 = bf16[64,8,2,2048]{3,2,1,0:T(2,128)(2,1)} all-to-all(bf16[64,8,2,2048]{3,2,1,0:T(2,128)(2,1)} %copy.94), channel_id=1, replica_groups=mesh['dp'=8,'expert'=64] {'expert'}, dimensions={0} | all-to-all | bytes 8388608 | tf_op jit(solution)/shard_map/all_to_all | solution.py:172
  412.6 7.3 %reshape.292 = bf16[1024,2048]{1,0:T(8,128)(2,1)} reshape(bf16[64,8,2,2048]{3,2,1,0:T(2,128)(2,1)} %all_to_all.46) | data formatting | bytes 8388608 | tf_op jit(solution)/shard_map/reshape | solution.py:173
  419.9 3.9 fusion.28
  423.8 2.3 fusion.2
  426.9 3.4 fusion.86
  430.3 0.7 all_to_all.37
  431.0 13.8 %all-to-all-start.2 = ((f32[64,1,16]{2,1,0:T(1,128)}), f32[64,1,16]{2,1,0:T(1,128)S(1)}, u32[]{:S(2)}, u32[]{:S(2)}) async-start(f32[64,1,16]{2,1,0:T(1,128)} %bitcast.28), calls=%async_computation.2 | async-start | bytes 65536 | tf_op jit(solution)/shard_map/all_to_all | solution.py:204
  444.9 14.2 %all-gather.8.cloned.1.call-done = bf16[1024,1408]{0,1:T(8,128)(2,1)} async-done(((bf16[1024,176]{0,1:T(8,128)(2,1)}), bf16[1024,1408]{0,1:T(8,128)(2,1)}) %all-gather.8.cloned.1.call-update) | async-done | bytes 2883600 | tf_op jit(solution)/shard_map/all_gather | solution.py:191
  459.1 3.6 convolution_convert_fusion
  462.8 15.3 %all-to-all-start.3 = ((bf16[64,16,256]{2,1,0:T(8,128)(2,1)}), bf16[64,16,256]{2,1,0:T(8,128)(2,1)S(1)}, u32[]{:S(2)}, u32[]{:S(2)}) async-start(bf16[64,16,256]{2,1,0:T(8,128)(2,1)} %bitcast.32), calls=%async_computation.3 | async-start | bytes 1048576 | tf_op jit(solution)/shard_map/all_to_all | solution.py:197
  478.1 3.0 fusion.82
  481.1 2.0 reshape_reshape.12
  483.1 3.8 reshape_reshape.11
  486.9 3.8 reshape_reshape.10
  490.6 1.0 reshape.320
  491.7 1.7 fusion.85
  493.4 1.7 fusion.11
  495.1 13.5 %all-gather.1 = bf16[8,176,136]{1,2,0:T(8,128)(2,1)S(1)} all-gather(bf16[1,176,136]{1,2,0:T(8,128)(2,1)S(1)} %fusion.11), channel_id=1, replica_groups=mesh['dp'=8,'expert'=64] {'dp'}, dimensions={0}, use_global_device_ids=true | all-gather | bytes 430848 | tf_op jit(solution)/shard_map/all_gather | solution.py:192
  508.7 1.2 reshape.322
  510.0 0.5 broadcast.221
  510.5 0.7 reduce.19
  511.3 3.5 gather_fusion
  515.3 3.4 gather_fusion.1
  518.9 0.5 multiply_reduce_fusion
  519.4 1.3 fusion.10
  520.7 8.1 %all_to_all.47 = bf16[8,17,256]{2,1,0:T(8,128)(2,1)S(1)} all-to-all(bf16[8,17,256]{2,1,0:T(8,128)(2,1)S(1)} %convert_element_type.163), channel_id=1, replica_groups=mesh['dp'=8,'expert'=64] {'dp'}, dimensions={0} | all-to-all | bytes 139264 | tf_op jit(solution)/shard_map/all_to_all | solution.py:221
  529.1 0.6 slice.80
  529.7 0.6 slice.79
  (88 shorter events, 3.7 us)
Async XLA Ops:
  7.2 452.0 %copy-start = (bf16[1,1408,256]{2,1,0:T(8,128)(2,1)S(1)}, bf16[1,1408,256]{2,1,0:T(8,128)(2,1)}, u32[]{:S(2)}) copy-start(bf16[1,1408,256]{2,1,0:T(8,128)(2,1)} %param.36) | copy-start | bytes 2162692
  7.2 14.1 %copy-start.7 = (f32[16]{0:T(128)S(1)}, f32[16]{0:T(128)}, u32[]{:S(2)}) copy-start(f32[16]{0:T(128)} %param.28) | copy-start | bytes 196
  7.2 14.1 %copy-start.12 = (bf16[16,576]{1,0:T(8,128)(2,1)S(1)}, bf16[16,576]{1,0:T(8,128)(2,1)}, u32[]{:S(2)}) copy-start(bf16[16,576]{1,0:T(8,128)(2,1)} %param.21) | copy-start | bytes 55300
  7.2 147.3 %all-gather.6.cloned.1.call-start = ((), (), s32[]{:S(2)}) async-start(), calls=%async_computation.5 | async-start | bytes 3594240 | tf_op jit(solution)/shard_map/all_gather | solution.py:43
  11.8 0.6 copy-start.4
  13.1 19.7 %copy-start.8 = (s32[17,6]{0,1:T(8,128)S(1)}, s32[17,6]{0,1:T(8,128)}, u32[]{:S(2)}) copy-start(s32[17,6]{0,1:T(8,128)} %param.33) | copy-start | bytes 1228
  22.6 28.4 %all-to-all-start = ((bf16[17,16,512]{2,0,1:T(8,128)(2,1)}), bf16[17,16,512]{2,0,1:T(8,128)(2,1)S(1)}, u32[]{:S(2)}, u32[]{:S(2)}) async-start(bf16[17,16,512]{2,0,1:T(8,128)(2,1)} %copy.83), calls=%async_computation | async-start | bytes 786432 | tf_op jit(solution)/shard_map/all_to_all | solution.py:141
  32.8 426.3 %all-gather.8.cloned.1.call-start = ((), (), s32[]{:S(2)}) async-start(), calls=%async_computation.6 | async-start | bytes 3244032 | tf_op jit(solution)/shard_map/all_gather | solution.py:191
  157.0 1.8 copy-start.2
  159.7 37.5 %copy-start.9 = (bf16[2048]{0:T(1024)(128)(2,1)S(1)}, bf16[2048]{0:T(1024)(128)(2,1)}, u32[]{:S(2)}) copy-start(bf16[2048]{0:T(1024)(128)(2,1)} %param.31) | copy-start | bytes 12292
  159.7 40.1 %copy-start.3 = (bf16[16,2048]{1,0:T(8,128)(2,1)S(1)}, bf16[16,2048]{1,0:T(8,128)(2,1)}, u32[]{:S(2)}) copy-start(bf16[16,2048]{1,0:T(8,128)(2,1)} %param.22) | copy-start | bytes 196612
  159.7 40.1 %copy-start.6 = (bf16[1,2048]{1,0:T(2,128)(2,1)S(1)}, bf16[1,2048]{1,0:T(2,128)(2,1)}, u32[]{:S(2)}) copy-start(bf16[1,2048]{1,0:T(2,128)(2,1)} %param.25) | copy-start | bytes 12292
  186.9 12.3 %collective-permute-start.1 = (bf16[24,2048]{1,0:T(8,128)(2,1)S(1)}, bf16[24,2048]{1,0:T(8,128)(2,1)S(1)}, u32[]{:S(2)}, u32[]{:S(2)}) collective-permute-start(bf16[24,2048]{1,0:T(8,128)(2,1)S(1)} %fusion), channel_id=1, source_target_pairs={{0,128},{64,192},{128,256},{192,320},{256,384},{320,448},{1,129},{... | collective-permute-start | bytes 294920
  188.2 11.0 %collective-permute-start = (bf16[24,2048]{1,0:T(8,128)(2,1)S(1)}, bf16[24,2048]{1,0:T(8,128)(2,1)S(1)}, u32[]{:S(2)}, u32[]{:S(2)}) collective-permute-start(bf16[24,2048]{1,0:T(8,128)(2,1)S(1)} %fusion), channel_id=1, source_target_pairs={{0,64},{64,128},{128,192},{192,256},{256,320},{320,384},{384,448},... | collective-permute-start | bytes 294920
  192.7 6.5 %collective-permute-start.2 = (bf16[1,2048]{1,0:T(2,128)(2,1)S(1)}, bf16[1,2048]{1,0:T(2,128)(2,1)S(1)}, u32[]{:S(2)}, u32[]{:S(2)}) collective-permute-start(bf16[1,2048]{1,0:T(2,128)(2,1)S(1)} %slice.81), channel_id=1, source_target_pairs={{0,192},{64,256},{128,320},{192,384},{256,448},{1,193},{65,257},{1... | collective-permute-start | bytes 12296
  412.6 7.3 %copy-start.10 = (bf16[1,2048,176]{1,2,0:T(8,128)(2,1)S(1)}, bf16[1,2048,176]{1,2,0:T(8,128)(2,1)}, u32[]{:S(2)}) copy-start(bf16[1,2048,176]{1,2,0:T(8,128)(2,1)} %param.34) | copy-start | bytes 2162692
  419.9 3.9 copy-start.1
  419.9 3.9 copy-start.11
  423.8 3.1 copy-start.5
  431.0 31.7 %all-to-all-start.2 = ((f32[64,1,16]{2,1,0:T(1,128)}), f32[64,1,16]{2,1,0:T(1,128)S(1)}, u32[]{:S(2)}, u32[]{:S(2)}) async-start(f32[64,1,16]{2,1,0:T(1,128)} %bitcast.28), calls=%async_computation.2 | async-start | bytes 65536 | tf_op jit(solution)/shard_map/all_to_all | solution.py:204
  462.8 52.5 %all-to-all-start.3 = ((bf16[64,16,256]{2,1,0:T(8,128)(2,1)}), bf16[64,16,256]{2,1,0:T(8,128)(2,1)S(1)}, u32[]{:S(2)}, u32[]{:S(2)}) async-start(bf16[64,16,256]{2,1,0:T(8,128)(2,1)} %bitcast.32), calls=%async_computation.3 | async-start | bytes 1048576 | tf_op jit(solution)/shard_map/all_to_all | solution.py:197
Sparse Core Ops, SparseCore 0:
  12.6 141.8 all-gather.5
  426.3 32.7 all-gather.7
where the time goes:
time: 539 us; the launch traced here: 537 us
  blocking collectives  265 us (49%)
  waiting for transfers between devices  118 us (22%)
  local copies, waits for them, and re-layouts  57.3 us (11%)
  starting transfers between devices  49.7 us (9%)
  matrix products  25.9 us (5%)
  between operations  16 us (3%)
  other arithmetic  6.09 us (1%)
    all_to_all x1, blocking collectives, shards(): lax.all_to_all(outgoing, 'expert', split_axis=0, concat_axis=0, tiled=True)  191 us
    all_gather x1, waiting for transfers between devices, gather_weights(): lax.all_gather(flat, 'expert', axis=0, tiled=True).reshape(members, padded)  103 us
    unnamed x1, blocking collectives  23.4 us
    all_to_all x1, starting transfers between devices, shards(): lax.all_to_all(expert_out.reshape(members, groups * capacity, col_width),...  15.3 us
    all_gather x1, blocking collectives, shards(): group_routes = lax.all_gather(routes, 'dp', axis=0, tiled=True)  14.7 us
    all_gather x1, waiting for transfers between devices, shards(): routed_piece = lax.all_gather(expert_act, 'dp', axis=1, tiled=True)  14.2 us
    all_to_all x1, starting transfers between devices, shards(): lax.all_to_all(gate_score.reshape(members, groups * capacity), 'expert',...  13.8 us
    all_gather x1, blocking collectives, shards(): group_tokens = lax.all_gather(normed, 'dp', axis=0, tiled=True)  13.8 us
  transfers between devices with their start and end apart: 8, of which 2 were waited for; matrix products, arithmetic and copies ran while one was open for 9% of the time, Pallas kernels for 0%

commit v1 on v0

--- a/solution.py
+++ b/solution.py
@@ -188,7 +188,9 @@
     ).astype(jnp.bfloat16)
     down_local = down_weight[0]
     col_width = down_local.shape[1]
-    routed_piece = lax.all_gather(expert_act, "dp", axis=1, tiled=True)
+    routed_piece = jnp.concatenate(
+        lax.all_to_all(jnp.stack([expert_act] * lax.axis_size("dp")), "dp", 0, 0), axis=1
+    )
     shared_piece = lax.all_gather(shared_act, "dp", axis=1, tiled=True)
     routed_cols = jnp.dot(routed_piece, down_local, preferred_element_type=jnp.float32)
     shared_cols = jnp.dot(shared_piece, shared_down_full, preferred_element_type=jnp.float32)

time: 539 us -> 561 us (1.041)
  waiting for transfers between devices: 118 us -> 143 us
    all_to_all x0 -> x1, waiting for transfers between devices: none -> 30.1 us  [shards(): lax.all_to_all(jnp.stack([expert_act] * lax.axis_size('dp')), 'dp', 0, 0)]
    all_gather x1 -> x0, waiting for transfers between devices: 14.2 us -> none  [shards(): routed_piece = lax.all_gather(expert_act, 'dp', axis=1, tiled=True)]
    all_to_all x0 -> x1, starting transfers between devices: none -> 10.9 us  [shards(): lax.all_to_all(jnp.stack([expert_act] * lax.axis_size('dp')), 'dp', 0, 0)]
    all_to_all x1, starting transfers between devices: 15.3 us -> 5 us  [shards(): lax.all_to_all(expert_out.reshape(members, groups * capacity, col_width),...]
    all_to_all x1, waiting for transfers between devices: 0.01 us -> 9.56 us  [shards(): lax.all_to_all(gate_score.reshape(members, groups * capacity), 'expert',...]
    all_to_all x1, starting transfers between devices: 13.8 us -> 7.7 us  [shards(): lax.all_to_all(gate_score.reshape(members, groups * capacity), 'expert',...]
  transfers between devices with their start and end apart: 8 -> 8, of which waited for: 2 -> 3; matrix products, arithmetic and copies ran while one was open for 9% -> 8% of each run, Pallas kernels for 0% -> 0%
where the time goes in v1:
time: 561 us; the launch traced here: 559 us
  blocking collectives  265 us (47%)
  waiting for transfers between devices  143 us (25%)
  local copies, waits for them, and re-layouts  59.3 us (11%)
  starting transfers between devices  44.2 us (8%)
  matrix products  25.2 us (4%)
  between operations  16 us (3%)
  other arithmetic  6.09 us (1%)
    all_to_all x1, blocking collectives, shards(): lax.all_to_all(outgoing, 'expert', split_axis=0, concat_axis=0, tiled=True)  191 us
    all_gather x1, waiting for transfers between devices, gather_weights(): lax.all_gather(flat, 'expert', axis=0, tiled=True).reshape(members, padded)  103 us
    all_to_all x1, waiting for transfers between devices, shards(): lax.all_to_all(jnp.stack([expert_act] * lax.axis_size('dp')), 'dp', 0, 0)  30.1 us
    unnamed x1, blocking collectives  23.4 us
    all_gather x1, blocking collectives, shards(): shared_piece = lax.all_gather(shared_act, 'dp', axis=1, tiled=True)  14.9 us
    all_gather x1, blocking collectives, shards(): group_routes = lax.all_gather(routes, 'dp', axis=0, tiled=True)  14.7 us
    all_gather x1, blocking collectives, shards(): group_tokens = lax.all_gather(normed, 'dp', axis=0, tiled=True)  13.8 us
    unnamed x41, local copies, waits for them, and re-layouts  11.2 us
  transfers between devices with their start and end apart: 8, of which 3 were waited for; matrix products, arithmetic and copies ran while one was open for 8% of the time, Pallas kernels for 0%

profile of v1, /device:TPU:1, one launch (start us, length us, event | category | flops | bytes accessed | tf_op | source)
XLA Modules:
  0.0 559.1 jit_solution(4560567723665931063)
XLA Ops:
  7.2 0.9 reshape.286
  8.1 0.8 reshape.287
  8.9 0.7 reshape.288
  9.7 0.7 copy.106
  10.4 0.7 bitcast_dynamic-update-slice_fusion
  11.8 0.6 copy-done.4
  13.2 1.7 fusion.83
  14.8 0.9 convert_convert_fusion
  15.9 1.6 fusion.84
  17.5 0.7 broadcast_maximum_fusion
  18.3 0.7 exponential_add_fusion.1
  18.9 0.7 slice_convert_fusion
  19.6 1.6 fusion.21
  21.7 0.9 copy.84
  22.6 10.2 %all-to-all-start = ((bf16[17,16,512]{2,0,1:T(8,128)(2,1)}), bf16[17,16,512]{2,0,1:T(8,128)(2,1)S(1)}, u32[]{:S(2)}, u32[]{:S(2)}) async-start(bf16[17,16,512]{2,0,1:T(8,128)(2,1)} %copy.84), calls=%async_computation | async-start | bytes 786432 | tf_op jit(solution)/shard_map/all_to_all | solution.py:141
  32.8 14.7 %all-gather.2 = s32[8,17,6]{1,2,0:T(8,128)S(1)} all-gather(s32[1,17,6]{1,2,0:T(8,128)S(1)} %bitcast.154), channel_id=1, replica_groups=mesh['dp'=8,'expert'=64] {'dp'}, dimensions={0}, use_global_device_ids=true | all-gather | bytes 3672 | tf_op jit(solution)/shard_map/all_gather | solution.py:161
  47.8 2.0 select_reduce_fusion
  50.0 1.0 slice_reduce_fusion.5
  51.3 103.2 %all-gather.5.cloned.1.call-done = bf16[64,212,128]{2,1,0:T(8,128)(2,1)} async-done(((bf16[1,212,128]{2,1,0:T(8,128)(2,1)}), bf16[64,212,128]{2,1,0:T(8,128)(2,1)}) %all-gather.5.cloned.1.call-update) | async-done | bytes 3473424 | tf_op jit(solution)/shard_map/all_gather | solution.py:43
  154.5 2.4 copy.121
  157.0 1.7 copy-done.2
  158.8 0.8 reshape.297
  159.7 1.7 copy.87
  161.4 1.5 reshape.298
  163.3 23.4 %fusion = bf16[24,2048]{1,0:T(8,128)(2,1)S(1)} fusion(bf16[136,2048]{1,0:T(8,128)(2,1)S(1)} %fusion.1), kind=kCustom, calls=%all-reduce-scatter | all-reduce-scatter fusion | flops 393217 | bytes 657408
  186.8 1.3 collective-permute-start.1
  188.1 4.5 collective-permute-start
  192.6 4.5 collective-permute-start.2
  197.1 1.3 dynamic-slice.4
  199.1 0.6 concatenate.12
  200.0 13.8 %all-gather = bf16[8,17,2048]{2,1,0:T(8,128)(2,1)S(1)} all-gather(bf16[1,17,2048]{2,1,0:T(8,128)(2,1)S(1)} %fusion.51), channel_id=1, replica_groups=mesh['dp'=8,'expert'=64] {'dp'}, dimensions={0}, use_global_device_ids=true | all-gather | bytes 626688 | tf_op jit(solution)/shard_map/all_gather | solution.py:160
  213.8 1.4 convolution_bitcast_fusion
  215.2 6.4 %copy.95 = bf16[64,8,2,2048]{3,2,1,0:T(2,128)(2,1)} copy(bf16[64,8,2,2048]{3,0,2,1:T(8,128)(2,1)S(1)} %convolution_bitcast_fusion) | data formatting | bytes 8388608 | tf_op jit(solution)/shard_map/grxc,grd->xgcd/transpose | solution.py:169
  221.6 191.1 %all_to_all.51 = bf16[64,8,2,2048]{3,2,1,0:T(2,128)(2,1)} all-to-all(bf16[64,8,2,2048]{3,2,1,0:T(2,128)(2,1)} %copy.95), channel_id=1, replica_groups=mesh['dp'=8,'expert'=64] {'expert'}, dimensions={0} | all-to-all | bytes 8388608 | tf_op jit(solution)/shard_map/all_to_all | solution.py:172
  412.6 7.3 %reshape.300 = bf16[1024,2048]{1,0:T(8,128)(2,1)} reshape(bf16[64,8,2,2048]{3,2,1,0:T(2,128)(2,1)} %all_to_all.51) | data formatting | bytes 8388608 | tf_op jit(solution)/shard_map/reshape | solution.py:173
  419.9 3.9 fusion.28
  423.8 1.6 fusion.2
  425.4 2.0 stack.2
  427.4 10.9 %all-to-all-start.3 = ((bf16[8,1024,176]{1,2,0:T(8,128)(2,1)}), bf16[8,1024,176]{1,2,0:T(8,128)(2,1)}, u32[]{:S(2)}, u32[]{:S(2)}) async-start(bf16[8,1024,176]{1,2,0:T(8,128)(2,1)} %stack.2), calls=%async_computation.3 | async-start | bytes 5767168 | tf_op jit(solution)/shard_map/all_to_all | solution.py:192
  439.1 3.4 fusion.86
  442.5 0.7 all_to_all.40
  443.2 30.1 %all-to-all-done.3 = bf16[8,1024,176]{1,2,0:T(8,128)(2,1)} async-done(((bf16[8,1024,176]{1,2,0:T(8,128)(2,1)}), bf16[8,1024,176]{1,2,0:T(8,128)(2,1)}, u32[]{:S(2)}, u32[]{:S(2)}) %all-to-all-start.3) | async-done | bytes 2883616 | tf_op jit(solution)/shard_map/all_to_all | solution.py:192
  473.2 7.7 %all-to-all-start.2 = ((f32[64,1,16]{2,1,0:T(1,128)}), f32[64,1,16]{2,1,0:T(1,128)S(1)}, u32[]{:S(2)}, u32[]{:S(2)}) async-start(f32[64,1,16]{2,1,0:T(1,128)} %bitcast.28), calls=%async_computation.2 | async-start | bytes 65536 | tf_op jit(solution)/shard_map/all_to_all | solution.py:206
  481.0 3.6 convolution_convert_fusion
  484.6 9.6 %all-to-all-done.2 = f32[64,1,16]{2,1,0:T(1,128)S(1)} async-done(((f32[64,1,16]{2,1,0:T(1,128)}), f32[64,1,16]{2,1,0:T(1,128)S(1)}, u32[]{:S(2)}, u32[]{:S(2)}) %all-to-all-start.2) | async-done | bytes 4128 | tf_op jit(solution)/shard_map/all_to_all | solution.py:206
  494.2 5.0 all-to-all-start.4
  499.2 2.9 fusion.82
  502.1 2.0 reshape_reshape.12
  504.1 3.8 reshape_reshape.11
  507.9 3.8 reshape_reshape.10
  511.7 1.0 reshape.330
  512.7 1.7 fusion.85
  514.4 1.7 fusion.11
  516.1 14.9 %all-gather.1 = bf16[8,176,136]{1,2,0:T(8,128)(2,1)S(1)} all-gather(bf16[1,176,136]{1,2,0:T(8,128)(2,1)S(1)} %fusion.11), channel_id=1, replica_groups=mesh['dp'=8,'expert'=64] {'dp'}, dimensions={0}, use_global_device_ids=true | all-gather | bytes 430848 | tf_op jit(solution)/shard_map/all_gather | solution.py:194
  531.2 1.2 reshape.332
  532.4 0.5 broadcast.223
  532.9 0.7 reduce.19
  533.7 3.5 gather_fusion
  537.7 3.4 gather_fusion.1
  541.3 0.5 multiply_reduce_fusion
  541.8 1.3 fusion.10
  543.1 7.7 %all_to_all.52 = bf16[8,17,256]{2,1,0:T(8,128)(2,1)S(1)} all-to-all(bf16[8,17,256]{2,1,0:T(8,128)(2,1)S(1)} %convert_element_type.163), channel_id=1, replica_groups=mesh['dp'=8,'expert'=64] {'dp'}, dimensions={0} | all-to-all | bytes 139264 | tf_op jit(solution)/shard_map/all_to_all | solution.py:223
  551.0 0.6 slice.80
  551.6 0.6 slice.79
  (88 shorter events, 4.9 us)
Async XLA Ops:
  7.2 473.8 %copy-start = (bf16[1,1408,256]{2,1,0:T(8,128)(2,1)S(1)}, bf16[1,1408,256]{2,1,0:T(8,128)(2,1)}, u32[]{:S(2)}) copy-start(bf16[1,1408,256]{2,1,0:T(8,128)(2,1)} %param.36) | copy-start | bytes 2162692
  7.2 14.1 %copy-start.7 = (f32[16]{0:T(128)S(1)}, f32[16]{0:T(128)}, u32[]{:S(2)}) copy-start(f32[16]{0:T(128)} %param.28) | copy-start | bytes 196
  7.2 14.1 %copy-start.12 = (bf16[16,576]{1,0:T(8,128)(2,1)S(1)}, bf16[16,576]{1,0:T(8,128)(2,1)}, u32[]{:S(2)}) copy-start(bf16[16,576]{1,0:T(8,128)(2,1)} %param.21) | copy-start | bytes 55300
  7.2 147.3 %all-gather.5.cloned.1.call-start = ((), (), s32[]{:S(2)}) async-start(), calls=%async_computation.6 | async-start | bytes 3594240 | tf_op jit(solution)/shard_map/all_gather | solution.py:43
  11.8 0.6 copy-start.4
  13.1 19.7 %copy-start.8 = (s32[17,6]{0,1:T(8,128)S(1)}, s32[17,6]{0,1:T(8,128)}, u32[]{:S(2)}) copy-start(s32[17,6]{0,1:T(8,128)} %param.33) | copy-start | bytes 1228
  22.6 28.4 %all-to-all-start = ((bf16[17,16,512]{2,0,1:T(8,128)(2,1)}), bf16[17,16,512]{2,0,1:T(8,128)(2,1)S(1)}, u32[]{:S(2)}, u32[]{:S(2)}) async-start(bf16[17,16,512]{2,0,1:T(8,128)(2,1)} %copy.84), calls=%async_computation | async-start | bytes 786432 | tf_op jit(solution)/shard_map/all_to_all | solution.py:141
  157.0 1.7 copy-start.2
  159.6 37.5 %copy-start.9 = (bf16[2048]{0:T(1024)(128)(2,1)S(1)}, bf16[2048]{0:T(1024)(128)(2,1)}, u32[]{:S(2)}) copy-start(bf16[2048]{0:T(1024)(128)(2,1)} %param.31) | copy-start | bytes 12292
  159.6 40.1 %copy-start.3 = (bf16[16,2048]{1,0:T(8,128)(2,1)S(1)}, bf16[16,2048]{1,0:T(8,128)(2,1)}, u32[]{:S(2)}) copy-start(bf16[16,2048]{1,0:T(8,128)(2,1)} %param.22) | copy-start | bytes 196612
  159.6 40.1 %copy-start.6 = (bf16[1,2048]{1,0:T(2,128)(2,1)S(1)}, bf16[1,2048]{1,0:T(2,128)(2,1)}, u32[]{:S(2)}) copy-start(bf16[1,2048]{1,0:T(2,128)(2,1)} %param.25) | copy-start | bytes 12292
  186.8 12.3 %collective-permute-start.1 = (bf16[24,2048]{1,0:T(8,128)(2,1)S(1)}, bf16[24,2048]{1,0:T(8,128)(2,1)S(1)}, u32[]{:S(2)}, u32[]{:S(2)}) collective-permute-start(bf16[24,2048]{1,0:T(8,128)(2,1)S(1)} %fusion), channel_id=1, source_target_pairs={{0,128},{64,192},{128,256},{192,320},{256,384},{320,448},{1,129},{... | collective-permute-start | bytes 294920
  188.1 11.0 %collective-permute-start = (bf16[24,2048]{1,0:T(8,128)(2,1)S(1)}, bf16[24,2048]{1,0:T(8,128)(2,1)S(1)}, u32[]{:S(2)}, u32[]{:S(2)}) collective-permute-start(bf16[24,2048]{1,0:T(8,128)(2,1)S(1)} %fusion), channel_id=1, source_target_pairs={{0,64},{64,128},{128,192},{192,256},{256,320},{320,384},{384,448},... | collective-permute-start | bytes 294920
  192.6 6.5 %collective-permute-start.2 = (bf16[1,2048]{1,0:T(2,128)(2,1)S(1)}, bf16[1,2048]{1,0:T(2,128)(2,1)S(1)}, u32[]{:S(2)}, u32[]{:S(2)}) collective-permute-start(bf16[1,2048]{1,0:T(2,128)(2,1)S(1)} %slice.81), channel_id=1, source_target_pairs={{0,192},{64,256},{128,320},{192,384},{256,448},{1,193},{65,257},{1... | collective-permute-start | bytes 12296
  412.6 7.3 %copy-start.10 = (bf16[1,2048,176]{1,2,0:T(8,128)(2,1)S(1)}, bf16[1,2048,176]{1,2,0:T(8,128)(2,1)}, u32[]{:S(2)}) copy-start(bf16[1,2048,176]{1,2,0:T(8,128)(2,1)} %param.34) | copy-start | bytes 2162692
  419.9 3.9 copy-start.1
  419.9 3.9 copy-start.11
  427.4 11.6 %copy-start.5 = (bf16[2048,1]{0,1:T(2,128)(2,1)S(1)}, bf16[2048,1]{0,1:T(2,128)(2,1)}, u32[]{:S(2)}) copy-start(bf16[2048,1]{0,1:T(2,128)(2,1)} %param.32) | copy-start | bytes 12292
  427.4 45.8 %all-to-all-start.3 = ((bf16[8,1024,176]{1,2,0:T(8,128)(2,1)}), bf16[8,1024,176]{1,2,0:T(8,128)(2,1)}, u32[]{:S(2)}, u32[]{:S(2)}) async-start(bf16[8,1024,176]{1,2,0:T(8,128)(2,1)} %stack.2), calls=%async_computation.3 | async-start | bytes 5767168 | tf_op jit(solution)/shard_map/all_to_all | solution.py:192
  473.2 20.9 %all-to-all-start.2 = ((f32[64,1,16]{2,1,0:T(1,128)}), f32[64,1,16]{2,1,0:T(1,128)S(1)}, u32[]{:S(2)}, u32[]{:S(2)}) async-start(f32[64,1,16]{2,1,0:T(1,128)} %bitcast.28), calls=%async_computation.2 | async-start | bytes 65536 | tf_op jit(solution)/shard_map/all_to_all | solution.py:206
  494.2 43.5 %all-to-all-start.4 = ((bf16[64,16,256]{2,1,0:T(8,128)(2,1)}), bf16[64,16,256]{2,1,0:T(8,128)(2,1)S(1)}, u32[]{:S(2)}, u32[]{:S(2)}) async-start(bf16[64,16,256]{2,1,0:T(8,128)(2,1)} %bitcast.34), calls=%async_computation.4 | async-start | bytes 1048576 | tf_op jit(solution)/shard_map/all_to_all | solution.py:199
Sparse Core Ops, SparseCore 0:
  12.6 141.8 all-gather.4
